TPU v7x, 256 devices: a whole 4x4x8 slice. The times are simulated.
256 devices in a mesh: row: 8 (over x, y_lo), col: 32 (over z, y_hi, core).
Axes of the slice: x: 4, y: 4 (y_hi: 2, y_lo: 2; y = y_hi * 2 + y_lo), z: 8, core: 2. Of those that a mesh axis runs over, the one named last changes fastest.
Arguments:
- prior_cov: float32 [4096, 4096], P('row', 'col'), as said below
- kernel: float32 [128, 2048], replicated, may hold values from -0.125 to 0.125
- offsets: int32 [128], replicated, may hold values from 0 to 2048
- obs_noise: float32 [128], replicated, may hold values from 64 to 512
- background: float32 [4096], P('col'), may hold values from -6 to 6
- observed: float32 [128], replicated, may hold values from -96 to 96
Outputs:
- analysis: float32 [4096], P('col')
- posterior: float32 [4096, 4096], P('row', 'col')
Inputs may be any that keep to these rules, and one draw needn't show every extreme that they name: prior_cov is exactly symmetric and positive definite.
All inputs are finite; a program needn't handle non-finite values.
Results may differ from a plain program's by a relative error of at most 0.0003.
Values sent between devices are 32-bit elements; how exact they have to be, the bound alone decides.
A program may use at most 64 MiB of HBM per device.

v0:
```python
import jax
import jax.numpy as jnp
from jax import lax
from jax.sharding import PartitionSpec as P

exact_mode = lax.Precision.HIGHEST


def from_root(block, axis, source):
    block = jnp.where(lax.axis_index(axis) == source, block, jnp.zeros_like(block))
    return lax.psum(block, axis)


def build_operator(kernel, offsets, first_state, states):
    support = kernel.shape[1]
    position = first_state + jnp.arange(states, dtype=jnp.int32)[None, :] - offsets[:, None]
    inside = (position >= 0) & (position < support)
    picked = jnp.take_along_axis(kernel, jnp.clip(position, 0, support - 1), axis=1)
    return jnp.where(inside, picked, jnp.zeros_like(picked))


def apply_inverse(inverse, right_side):
    return jnp.dot(inverse, right_side, precision=exact_mode, preferred_element_type=jnp.float32)


def on_device(prior_cov, kernel, offsets, obs_noise, background, observed):
    row_states, col_states = prior_cov.shape
    per_row = lax.axis_size("col") // lax.axis_size("row")
    col_index = lax.axis_index("col")
    col_operator = build_operator(kernel, offsets, col_index * col_states, col_states)
    partial_value = lax.dot_general(
        col_operator,
        prior_cov,
        (((1,), (1,)), ((), ())),
        precision=exact_mode,
        preferred_element_type=jnp.float32,
    )
    row_image = lax.psum(partial_value, "col")
    within = col_index % per_row * col_states
    panel_part = lax.dynamic_slice_in_dim(row_image, within, col_states, 1)
    col_image = from_root(panel_part, "row", col_index // per_row)
    innov_part = lax.dot_general(
        col_image,
        col_operator,
        (((1,), (1,)), ((), ())),
        precision=exact_mode,
        preferred_element_type=jnp.float32,
    )
    mean_part = jnp.dot(
        col_operator, background, precision=exact_mode, preferred_element_type=jnp.float32
    )
    innov_sum, mean_sum = lax.psum((innov_part, mean_part), "col")
    innov_cov = innov_sum + jnp.diag(obs_noise)
    innovation = observed - mean_sum
    factor = jnp.linalg.cholesky(innov_cov)
    identity = jnp.eye(factor.shape[0], dtype=jnp.float32)
    inverse = lax.linalg.triangular_solve(factor, identity, left_side=True, lower=True)
    col_white = apply_inverse(inverse, col_image)
    weights = apply_inverse(inverse, innovation)
    analysis = background + jnp.dot(
        weights, col_white, precision=exact_mode, preferred_element_type=jnp.float32
    )
    row_white = apply_inverse(inverse, row_image)
    downdate = lax.dot_general(
        row_white,
        col_white,
        (((0,), (0,)), ((), ())),
        precision=exact_mode,
        preferred_element_type=jnp.float32,
    )
    posterior = prior_cov - downdate
    return (analysis, posterior)


def solution(mesh):
    placed = (P("row", "col"), P(), P(), P(), P("col"), P())
    return jax.shard_map(
        on_device,
        mesh=mesh,
        in_specs=placed,
        out_specs=(P("col"), P("row", "col")),
        check_vma=False,
    )
```

profile of v0, /device:TPU:1, one launch (start us, length us, event | category | flops | bytes accessed | tf_op | source)
XLA Modules:
  0.0 767.0 jit_solution(12935860035592293265)
XLA Ops:
  7.2 0.0 copy-start
  7.2 0.0 all-reduce.4.cloned.1.call-start
  7.2 0.8 fusion.7
  8.1 0.3 copy-done
  8.4 129.5 %gather_fusion = f32[16384]{0:T(1024)S(1)} fusion(f32[128,2048]{1,0:T(8,128)S(1)} %copy-done, s32[16384]{0:T(1024)S(1)} %fusion.7), kind=kCustom, calls=%fused_computation | custom fusion | bytes 262144 | tf_op jit(solution)/shard_map/jit(take_along_axis)/gather | solution.py:18
  137.9 0.0 copy-start.7
  137.9 1.1 fusion.17
  139.1 0.0 all-reduce.4.cloned.1.call-update
  139.1 0.0 all-reduce.6.cloned.1.call-start
  139.2 274.3 %all-reduce.4.cloned.1.call-done = f32[128,512]{1,0:T(8,128)} async-done(((f32[128,512]{1,0:T(8,128)}), f32[128,512]{1,0:T(8,128)}) %all-reduce.4.cloned.1.call-update) | async-done | bytes 262160 | tf_op jit(solution)/shard_map/psum | solution.py:38
  413.5 1.5 dynamic-slice_select_fusion
  415.1 0.0 all-reduce.6.cloned.1.call-update
  415.1 0.0 all-reduce.8.cloned.1.call-start
  415.1 74.0 %all-reduce.6.cloned.1.call-done = f32[128,128]{1,0:T(8,128)} async-done(((f32[128,128]{1,0:T(8,128)}), f32[128,128]{1,0:T(8,128)}) %all-reduce.6.cloned.1.call-update) | async-done | bytes 65552 | tf_op jit(solution)/shard_map/psum | solution.py:11
  489.2 1.9 fusion.15
  491.1 0.0 all-reduce.8.cloned.1.call-update
  491.1 0.3 convolution_bitcast_fusion.2
  491.4 70.5 %psum.31 = f32[128]{0:T(128)S(1)} all-reduce(f32[128]{0:T(128)S(1)} %convolution_bitcast_fusion.2), channel_id=1, replica_groups=mesh['row'=8,'col'=32] {'col'}, use_global_device_ids=true, to_apply=%region_5.6 | all-reduce | flops 128 | bytes 1024 | tf_op jit(solution)/shard_map/psum | solution.py:52
  561.9 170.7 %all-reduce.8.cloned.1.call-done = f32[128,128]{1,0:T(8,128)} async-done(((f32[128,128]{1,0:T(8,128)}), f32[128,128]{1,0:T(8,128)}) %all-reduce.8.cloned.1.call-update) | async-done | bytes 65552 | tf_op jit(solution)/shard_map/psum | solution.py:52
  732.6 0.9 select_add_fusion
  733.5 0.1 copy.9
  733.6 0.9 fusion.10
  734.5 11.7 %cholesky.16 = f32[128,128]{1,0:T(8,128)S(1)} custom-call(f32[128,128]{1,0:T(8,128)S(1)} %fusion.10), custom_call_target="Cholesky" | custom-call | tf_op jit(solution)/shard_map/jit(cholesky)/cholesky | solution.py:55
  746.3 0.6 compare_reduce_fusion
  746.9 0.7 fusion.1
  747.6 9.8 %custom-call.6 = f32[1,128,128]{1,2,0:T(8,128)S(1)} custom-call(f32[1,128,128]{2,1,0:T(8,128)S(1)} %fusion.1), custom_call_target="InvertDiagBlocksLowerTriangular" | custom-call | tf_op jit(solution)/shard_map/triangular_solve | solution.py:57
  757.4 0.2 fusion.8
  757.6 0.2 convolution_bitcast_fusion.1
  757.8 0.2 fusion.37
  758.1 0.7 fusion
  758.8 0.4 fusion.38
  759.1 1.3 convolution_subtract_fusion
  (15 shorter events, 0.1 us)
Async XLA Ops:
  7.2 1.2 copy-start
  7.2 406.3 %all-reduce.4.cloned.1.call-start = ((), (), s32[]{:S(2)}) async-start(), calls=%async_computation | async-start | bytes 524288 | tf_op jit(solution)/shard_map/psum | solution.py:38
  8.4 129.5 %copy-start.1 = (f32[512,128]{1,0:T(8,128)S(1)}, f32[512,128]{1,0:T(8,128)}, u32[]{:S(2)}) copy-start(f32[512,128]{1,0:T(8,128)} %param.6) | copy-start | bytes 786436
  8.4 129.5 %copy-start.4 = (s32[128]{0:T(128)S(1)}, s32[128]{0:T(128)}, u32[]{:S(2)}) copy-start(s32[128]{0:T(128)} %param.8) | copy-start | bytes 1540
  137.9 353.2 %copy-start.7 = (f32[128]{0:T(128)S(1)}, f32[128]{0:T(128)}, u32[]{:S(2)}) copy-start(f32[128]{0:T(128)} %param.10) | copy-start | bytes 1540
  137.9 594.6 %copy-start.5 = (f32[128]{0:T(128)S(1)}, f32[128]{0:T(128)}, u32[]{:S(2)}) copy-start(f32[128]{0:T(128)} %param.9) | copy-start | bytes 1540
  139.1 618.6 %copy-start.6 = (f32[128]{0:T(128)S(1)}, f32[128]{0:T(128)}, u32[]{:S(2)}) copy-start(f32[128]{0:T(128)} %param.11) | copy-start | bytes 1540
  139.1 350.1 %all-reduce.6.cloned.1.call-start = ((), (), s32[]{:S(2)}) async-start(), calls=%async_computation.1 | async-start | bytes 131072 | tf_op jit(solution)/shard_map/psum | solution.py:11
  413.5 345.2 %copy-start.2 = (f32[128,512]{1,0:T(8,128)S(1)}, f32[128,512]{1,0:T(8,128)}, u32[]{:S(2)}) copy-start(f32[128,512]{1,0:T(8,128)} %all-reduce.4.cloned.1.call-done) | copy-start | bytes 786436
  415.1 317.5 %all-reduce.8.cloned.1.call-start = ((), (), s32[]{:S(2)}) async-start(), calls=%async_computation.2 | async-start | bytes 131072 | tf_op jit(solution)/shard_map/psum | solution.py:52
  489.2 268.7 %copy-start.3 = (f32[128,128]{1,0:T(8,128)S(1)}, f32[128,128]{1,0:T(8,128)}, u32[]{:S(2)}) copy-start(f32[128,128]{1,0:T(8,128)} %all-reduce.6.cloned.1.call-done) | copy-start | bytes 196612
Sparse Core Ops, SparseCore 0:
  139.2 274.2 all-reduce.3
  416.7 72.4 all-reduce.5
  492.4 240.1 all-reduce.7
where the time goes:
time: 768 us; the launch traced here: 767 us
  waiting for transfers between devices  519 us (68%)
  local copies, waits for them, and re-layouts  130 us (17%)
  blocking collectives  70.5 us (9%)
  other arithmetic  27.1 us (4%)
  between operations  13.9 us (2%)
    psum x1, waiting for transfers between devices, on_device(): row_image = lax.psum(partial_value, 'col')  274 us
    psum x1, waiting for transfers between devices, on_device(): innov_sum, mean_sum = lax.psum((innov_part, mean_part), 'col')  171 us
    gather x1, local copies, waits for them, and re-layouts, build_operator(): jnp.take_along_axis(kernel, jnp.clip(position, 0, support - 1), axis=1)  129 us
    psum x1, waiting for transfers between devices, from_root(): return lax.psum(block, axis)  74 us
    psum x1, blocking collectives, on_device(): innov_sum, mean_sum = lax.psum((innov_part, mean_part), 'col')  70.5 us
  transfers between devices with their start and end apart: 3, of which 3 were waited for; matrix products, arithmetic and copies ran while one was open for 0% of the time, Pallas kernels for 0%

commit v1 on v0

v1 whole, which is shorter than its diff:
```python
import jax
import jax.numpy as jnp
from jax import lax
from jax.experimental import pallas as pl
from jax.experimental.pallas import tpu as pltpu
from jax.sharding import PartitionSpec as P

MESH = pl.DeviceIdType.MESH
F32 = jnp.float32
BF16 = jnp.bfloat16
M = 128
LOW = 24
CHUNKS = 64
PIVOTS = 16


def mm(a, b):
    return jnp.dot(a, b, precision=lax.Precision.HIGHEST, preferred_element_type=F32)


def mm_nt(a, b):
    return lax.dot_general(
        a, b, (((1,), (1,)), ((), ())), precision=lax.Precision.HIGHEST, preferred_element_type=F32
    )


def split(a):
    high = a.astype(BF16)
    return high, (a - high.astype(F32)).astype(BF16)


def row_of(x, p):
    return jnp.broadcast_to(x[p : p + 1, :], x.shape)


def col_of(x, j):
    return jnp.broadcast_to(x[:, j : j + 1], x.shape)


def spd_inverse(blocks, b):
    count = M // b
    lane = lax.broadcasted_iota(jnp.int32, (b, M), 1)
    sub = lax.broadcasted_iota(jnp.int32, (b, M), 0)
    ahead = blocks[0]
    for k in range(count):
        inside = (lane >= k * b) & (lane < (k + 1) * b)
        cols = [col_of(ahead, k * b + j) for j in range(b)]
        top = jnp.where(inside, jnp.where(lane - k * b == sub, 1.0, 0.0), ahead)
        for p in range(b):
            scale = 1.0 / row_of(cols[p], p)
            is_p = sub == p
            t = row_of(top, p) * scale
            top = jnp.where(is_p, t, top - cols[p] * t)
            for j in range(p + 1, b):
                t = row_of(cols[j], p) * scale
                cols[j] = jnp.where(is_p, t, cols[j] - cols[p] * t)
        following = None
        if k + 1 < count:
            old = blocks[k + 1]
            following = jnp.where(inside, 0.0, old)
            for j in range(b):
                following = following - col_of(old, k * b + j) * row_of(top, j)
        if k + 1 < count or count > 1:
            a_hi, a_lo = split(jnp.concatenate(blocks, 0))
            t_hi, t_lo = split(top)

            def placed(t):
                parts = [t.astype(F32)]
                if k:
                    parts.insert(0, jnp.zeros((k * b, M), F32))
                if k + 1 < count:
                    parts.append(jnp.zeros((M - (k + 1) * b, M), F32))
                return jnp.concatenate(parts, 0).astype(BF16)

            t_hi, t_lo = placed(t_hi), placed(t_lo)
            update = (
                jnp.dot(a_hi, t_hi, preferred_element_type=F32)
                + jnp.dot(a_lo, t_hi, preferred_element_type=F32)
                + jnp.dot(a_hi, t_lo, preferred_element_type=F32)
            )
        new = []
        for i in range(count):
            if i == k:
                new.append(top)
            elif i == k + 1:
                new.append(following)
            else:
                new.append(jnp.where(inside, 0.0, blocks[i]) - update[i * b : (i + 1) * b])
        blocks, ahead = new, following
    return jnp.concatenate(blocks, 0)


def tree_sum(terms):
    while len(terms) > 1:
        terms = [sum(terms[i : i + 2][1:], terms[i]) for i in range(0, len(terms), 2)]
    return terms[0]


def kernel(
    prior_hbm, kernel_hbm, off_ref, noise_ref, bg_ref, obs_ref,
    ana_ref, post_hbm,
    kpad, hall, pv, outv,
    s_src, s_rs, z_src, z_rs, s_fin,
    m_src, m_rs, m2_src, m2_rs,
    g_src, g_rs, g_sl, g_col, g_row,
    load_sem, out_sem,
    s_send, s_recv, z_send, z_recv, f_send, f_recv,
    m_send, m_recv, m2_send, m2_recv, gs_send, gs_recv, gc_send, gc_recv, gr_send, gr_recv,
):
    r = lax.axis_index("row")
    c = lax.axis_index("col")
    z = c // 4
    y_hi = (c // 2) % 2
    core = c % 2
    q = r * 2 + y_hi
    w = z * 2 + core

    def plane(i):
        return (i // 2, z * 4 + (i % 2) * 2 + core)

    def column(i):
        return (r, (i // 2) * 4 + y_hi * 2 + i % 2)

    barrier = pltpu.get_barrier_semaphore()

    @pl.loop(1, 16)
    def _(i):
        pl.semaphore_signal(barrier, inc=1, device_id=plane((q + i) % 16), device_id_type=MESH)
        pl.semaphore_signal(barrier, inc=1, device_id=column((w + i) % 16), device_id_type=MESH)

    for k in range(16):
        pltpu.make_async_copy(
            kernel_hbm.at[:, pl.ds(k * 128, 128)], kpad.at[pl.ds((LOW + k) * 128, 128)], load_sem.at[0]
        ).start()
    prior_copy = pltpu.make_async_copy(prior_hbm, pv, load_sem.at[1])
    prior_copy.start()
    zeros = jnp.zeros((128, 128), F32)
    for start, stop in ((0, LOW), (LOW + 16, CHUNKS)):
        @pl.loop(start, stop)
        def _(i):
            kpad[pl.ds(pl.multiple_of(i * 128, 128), 128), :] = zeros

    data = kpad.at[pl.ds(LOW * 128, 16 * 128)]
    pltpu.make_async_copy(data, data, load_sem.at[0]).wait()

    lane = lax.broadcasted_iota(jnp.int32, (8, 128), 1)
    sub = lax.broadcasted_iota(jnp.int32, (8, 128), 0)

    def build(m, carry):
        off = off_ref[m]
        chunk = lax.shift_right_logical(off, 7)
        turn = lax.bitwise_and(off, 127)
        at_r = (LOW + 4 * r - chunk) * 128 + m
        at_c = (LOW + c - chunk) * 128 + m
        now = jnp.where(
            sub < 4, kpad[pl.ds(at_r, 8, stride=128), :], jnp.broadcast_to(kpad[pl.ds(at_c, 1), :], (8, 128))
        )
        before = jnp.where(
            sub < 4,
            kpad[pl.ds(at_r - 128, 8, stride=128), :],
            jnp.broadcast_to(kpad[pl.ds(at_c - 128, 1), :], (8, 128)),
        )
        turned = pltpu.roll(jnp.where(lane >= 128 - turn, before, now), turn, axis=1)
        hall[pl.ds(m, 8, stride=128), :] = turned
        return carry

    lax.fori_loop(0, M, build, 0, unroll=8)

    prior_copy.wait()
    part = mm(hall[0:128, :], pv[0:128, :])
    for j in range(1, 4):
        part += mm(hall[j * 128 : (j + 1) * 128, :], pv[j * 128 : (j + 1) * 128, :])
    h_c = hall[512:640, :]
    s_part = mm_nt(h_c, part)
    s_src[...] = s_part.reshape(16, 8, 128)
    s_rs[q] = s_src[q]

    pl.semaphore_wait(barrier, 30)

    @pl.loop(1, 16)
    def _(i):
        to = (q + i) % 16
        pltpu.make_async_remote_copy(
            s_src.at[to], s_rs.at[q], s_send, s_recv, device_id=plane(to), device_id_type=MESH
        ).start()

    g_src[...] = jnp.transpose(part).reshape(8, 16, 128)
    g_rs[r] = g_src[r]

    @pl.loop(1, 8)
    def _(i):
        to = (r + i) % 8
        pltpu.make_async_remote_copy(
            g_src.at[to], g_rs.at[r], gs_send, gs_recv, device_id=(to, c), device_id_type=MESH
        ).start()

    bg8 = jnp.broadcast_to(bg_ref[...], (8, 128))
    mean = mm_nt(bg8, h_c)
    m_src[0] = mean
    m_rs[w] = mean

    @pl.loop(1, 16)
    def _(i):
        pltpu.make_async_remote_copy(
            m_src.at[0], m_rs.at[w], m_send, m_recv, device_id=column((w + i) % 16), device_id_type=MESH
        ).start()

    def arrived(buffer, count, send, recv):
        view = buffer.at[pl.ds(0, count)]
        return pltpu.make_async_remote_copy(view, view, send, recv, device_id=(r, c), device_id_type=MESH)

    arrived(s_rs, 15, s_send, s_recv).wait_recv()
    tile = tree_sum([s_rs[i] for i in range(16)])
    z_src[0] = tile
    z_rs[w] = tile

    @pl.loop(1, 16)
    def _(i):
        pltpu.make_async_remote_copy(
            z_src.at[0], z_rs.at[w], z_send, z_recv, device_id=column((w + i) % 16), device_id_type=MESH
        ).start()

    arrived(g_rs, 7, gs_send, gs_recv).wait_recv()
    g_sl[0] = tree_sum([g_rs[i] for i in range(8)])

    arrived(m_rs, 15, m_send, m_recv).wait_recv()
    mean = tree_sum([m_rs[i] for i in range(16)])
    m2_src[0] = mean

    arrived(z_rs, 15, z_send, z_recv).wait_recv()
    tile = tree_sum([z_rs[i] for i in range(16)])
    s_fin[q] = tile
    z_src[1] = tile

    @pl.loop(1, 16)
    def _(i):
        pltpu.make_async_remote_copy(
            z_src.at[1], s_fin.at[q], f_send, f_recv, device_id=plane((q + i) % 16), device_id_type=MESH
        ).start()

    other = r * 2 + 1 - y_hi
    mean_copy = pltpu.make_async_remote_copy(
        m2_src, m2_rs, m2_send, m2_recv, device_id=plane(other), device_id_type=MESH
    )
    mean_copy.start()

    arrived(s_fin, 15, f_send, f_recv).wait_recv()

    @pl.loop(1, 8)
    def _(i):
        pltpu.make_async_remote_copy(
            g_sl.at[0], g_col.at[r], gc_send, gc_recv, device_id=((r + i) % 8, c), device_id_type=MESH
        ).start()

    slot = (c % 4) * 8 + r

    @pl.loop(1, 32)
    def _(i):
        pltpu.make_async_remote_copy(
            g_sl.at[0], g_row.at[slot], gr_send, gr_recv, device_id=(z, (c + i) % 32), device_id_type=MESH
        ).start()

    @pl.when(z == r)
    def _():
        pltpu.make_async_copy(g_sl.at[0], g_row.at[slot], gr_recv).start()

    @pl.when(z != r)
    def _():
        pltpu.make_async_remote_copy(
            g_sl.at[0], g_row.at[slot], gr_send, gr_recv, device_id=(z, c), device_id_type=MESH
        ).start()

    g_col[r] = g_sl[0]

    s_all = s_fin[...].reshape(128, 128)
    rows = lax.broadcasted_iota(jnp.int32, (128, 128), 0)
    lanes = lax.broadcasted_iota(jnp.int32, (128, 128), 1)
    s_all = s_all + jnp.where(rows == lanes, jnp.broadcast_to(noise_ref[...], (128, 128)), 0.0)
    inverse = spd_inverse([s_all[i * PIVOTS : (i + 1) * PIVOTS] for i in range(M // PIVOTS)], PIVOTS)

    arrived(g_col, 7, gc_send, gc_recv).wait_recv()
    solved = mm(g_col[...].reshape(128, 128), inverse)

    mean_copy.wait_recv()
    mean = m2_src[0] + m2_rs[0]
    innovation = jnp.broadcast_to(obs_ref[...], (8, 128)) - mean
    ana_ref[...] = bg_ref[...] + mm_nt(innovation, solved)[0:1, :]

    arrived(g_row, 32, gr_send, gr_recv).wait_recv()
    for j in range(4):
        g_j = g_row[j * 8 : (j + 1) * 8].reshape(128, 128)
        outv[j] = pv[j * 128 : (j + 1) * 128, :] - mm_nt(g_j, solved)
        pltpu.make_async_copy(outv.at[j], post_hbm.at[pl.ds(j * 128, 128)], out_sem.at[j]).start()

    arrived(s_rs, 15, s_send, s_recv).wait_send()
    arrived(z_rs, 15, z_send, z_recv).wait_send()
    arrived(s_fin, 15, f_send, f_recv).wait_send()
    arrived(m_rs, 15, m_send, m_recv).wait_send()
    arrived(g_rs, 7, gs_send, gs_recv).wait_send()
    arrived(g_col, 7, gc_send, gc_recv).wait_send()
    mean_copy.wait_send()

    @pl.when(z == r)
    def _():
        arrived(g_row, 31, gr_send, gr_recv).wait_send()

    @pl.when(z != r)
    def _():
        arrived(g_row, 32, gr_send, gr_recv).wait_send()

    for j in range(4):
        pltpu.make_async_copy(outv.at[j], post_hbm.at[pl.ds(j * 128, 128)], out_sem.at[j]).wait()


def on_device(prior_cov, kern, offsets, obs_noise, background, observed):
    vmem = pl.BlockSpec(memory_space=pltpu.VMEM)
    hbm = pl.BlockSpec(memory_space=pl.ANY)
    dma = pltpu.SemaphoreType.DMA
    ana, post = pl.pallas_call(
        kernel,
        name="analysis",
        out_shape=(jax.ShapeDtypeStruct((1, 128), F32), jax.ShapeDtypeStruct((512, 128), F32)),
        in_specs=[hbm, hbm, pl.BlockSpec(memory_space=pltpu.SMEM), vmem, vmem, vmem],
        out_specs=(vmem, hbm),
        scratch_shapes=[
            pltpu.VMEM((CHUNKS * 128, 128), F32),
            pltpu.VMEM((8 * 128, 128), F32),
            pltpu.VMEM((512, 128), F32),
            pltpu.VMEM((4, 128, 128), F32),
            pltpu.VMEM((16, 8, 128), F32),
            pltpu.VMEM((16, 8, 128), F32),
            pltpu.VMEM((2, 8, 128), F32),
            pltpu.VMEM((16, 8, 128), F32),
            pltpu.VMEM((16, 8, 128), F32),
            pltpu.VMEM((1, 8, 128), F32),
            pltpu.VMEM((16, 8, 128), F32),
            pltpu.VMEM((1, 8, 128), F32),
            pltpu.VMEM((1, 8, 128), F32),
            pltpu.VMEM((8, 16, 128), F32),
            pltpu.VMEM((8, 16, 128), F32),
            pltpu.VMEM((1, 16, 128), F32),
            pltpu.VMEM((8, 16, 128), F32),
            pltpu.VMEM((32, 16, 128), F32),
            dma((2,)),
            dma((4,)),
        ]
        + [dma] * 16,
        compiler_params=pltpu.CompilerParams(
            collective_id=0, has_side_effects=True, vmem_limit_bytes=32 * 1024 * 1024
        ),
    )(
        prior_cov,
        kern,
        offsets,
        obs_noise.reshape(1, 128),
        background.reshape(1, 128),
        observed.reshape(1, 128),
    )
    return ana.reshape(128), post


def solution(mesh):
    placed = (P("row", "col"), P(), P(), P(), P("col"), P())
    return jax.shard_map(
        on_device,
        mesh=mesh,
        in_specs=placed,
        out_specs=(P("col"), P("row", "col")),
        check_vma=False,
    )
```

time: 768 us -> 41.2 us (0.05)
  the two profiles are of different devices: /device:TPU:1 before, /device:TPU:3 now
where the time goes in v1:
time: 41.2 us; the launch traced here: 41 us
  Pallas kernels  36.3 us (88%)
  local copies, waits for them, and re-layouts  4.06 us (10%)
  between operations  0.68 us (2%)
    pallas_call x1, Pallas kernels, on_device(): pl.pallas_call(kernel, name='analysis', out_shape=(jax.ShapeDtypeStruct((...  36.3 us
    unnamed x14, local copies, waits for them, and re-layouts  4.06 us

profile of v1, /device:TPU:3, one launch (start us, length us, event | category | flops | bytes accessed | tf_op | source)
XLA Modules:
  0.0 41.0 jit_solution(6537255979479490043)
XLA Ops:
  0.6 0.0 copy-start.5
  0.6 0.0 copy-start.2
  0.7 0.0 copy-start.3
  0.7 0.0 copy-start.4
  0.7 0.6 %copy-done.5 = f32[128]{0:T(128)S(1)} copy-done((f32[128]{0:T(128)S(1)}, f32[128]{0:T(128)}, u32[]{:S(2)}) %copy-start.5) | copy-done | bytes 536
  1.3 0.0 copy-done.2
  1.3 0.0 copy-done.3
  1.3 0.0 copy-done.4
  1.3 0.0 copy-start
  1.3 1.2 %copy-done = f32[128,2048]{1,0:T(8,128)S(1)} copy-done((f32[128,2048]{1,0:T(8,128)S(1)}, f32[128,2048]{1,0:T(8,128)}, u32[]{:S(2)}) %copy-start) | copy-done | bytes 1048600
  2.6 0.0 copy-start.1
  2.6 0.9 %copy-done.1 = f32[512,128]{1,0:T(8,128)S(1)} copy-done((f32[512,128]{1,0:T(8,128)S(1)}, f32[512,128]{1,0:T(8,128)}, u32[]{:S(2)}) %copy-start.1) | copy-done | bytes 262168
  3.5 36.3 %analysis.1 = (f32[1,128]{1,0:T(1,128)S(1)}, f32[512,128]{1,0:T(8,128)S(1)}) custom-call(f32[512,128]{1,0:T(8,128)S(1)} %copy-done.1, f32[128,2048]{1,0:T(8,128)S(1)} %copy-done, s32[128]{0:T(128)S(1)} %copy-done.2, f32[1,128]{1,0:T(1,128)S(1)} %bitcast.4, f32[1,128]{1,0:T(1,128)S(1)} %bitcast.5, f32[1,128]{1,0:T(1,128)S(1)} %bitcast.6), custom_call_target="tpu_custom_call" | custom-call | tf_op jit(solution)/shard_map/analysis/pallas_call | solution.py:319
  39.8 0.5 %copy.10 = f32[128]{0:T(128)} copy(f32[128]{0:T(128)S(1)} %bitcast.7) | data formatting | bytes 1024
  40.3 0.7 %copy.11 = f32[512,128]{1,0:T(8,128)} copy(f32[512,128]{1,0:T(8,128)S(1)} %get-tuple-element.9) | data formatting | bytes 524288
Async XLA Ops:
  0.6 0.7 %copy-start.5 = (f32[128]{0:T(128)S(1)}, f32[128]{0:T(128)}, u32[]{:S(2)}) copy-start(f32[128]{0:T(128)} %param.11) | copy-start | bytes 1540
  0.6 0.7 %copy-start.2 = (s32[128]{0:T(128)S(1)}, s32[128]{0:T(128)}, u32[]{:S(2)}) copy-start(s32[128]{0:T(128)} %off_ref.1) | copy-start | bytes 1540
  0.7 0.7 %copy-start.3 = (f32[128]{0:T(128)S(1)}, f32[128]{0:T(128)}, u32[]{:S(2)}) copy-start(f32[128]{0:T(128)} %param.9) | copy-start | bytes 1540
  0.7 0.7 %copy-start.4 = (f32[128]{0:T(128)S(1)}, f32[128]{0:T(128)}, u32[]{:S(2)}) copy-start(f32[128]{0:T(128)} %param.10) | copy-start | bytes 1540
  1.3 1.2 %copy-start = (f32[128,2048]{1,0:T(8,128)S(1)}, f32[128,2048]{1,0:T(8,128)}, u32[]{:S(2)}) copy-start(f32[128,2048]{1,0:T(8,128)} %kernel_hbm.1) | copy-start | bytes 3145732
  2.6 0.9 %copy-start.1 = (f32[512,128]{1,0:T(8,128)S(1)}, f32[512,128]{1,0:T(8,128)}, u32[]{:S(2)}) copy-start(f32[512,128]{1,0:T(8,128)} %prior_hbm.1) | copy-start | bytes 786436

commit v2 on v1

v2 whole, which is shorter than its diff:
```python
import jax
import jax.numpy as jnp
from jax import lax
from jax.experimental import pallas as pl
from jax.experimental.pallas import tpu as pltpu
from jax.sharding import PartitionSpec as P

MESH = pl.DeviceIdType.MESH
F32 = jnp.float32
M = 128
LOW = 24
CHUNKS = 64
STRIDE = 136
GROUP = 32
PIVOTS = 16


def mm(a, b):
    return jnp.dot(a, b, precision=lax.Precision.HIGHEST, preferred_element_type=F32)


def mm_nt(a, b):
    return lax.dot_general(
        a, b, (((1,), (1,)), ((), ())), precision=lax.Precision.HIGHEST, preferred_element_type=F32
    )


def row_of(x, p):
    return jnp.broadcast_to(x[p : p + 1, :], x.shape)


def col_of(x, j):
    return jnp.broadcast_to(x[:, j : j + 1], x.shape)


def spd_inverse(blocks, b):
    count = M // b
    lane = lax.broadcasted_iota(jnp.int32, (b, M), 1)
    sub = lax.broadcasted_iota(jnp.int32, (b, M), 0)
    ahead = blocks[0]
    for k in range(count):
        inside = (lane >= k * b) & (lane < (k + 1) * b)
        cols = [col_of(ahead, k * b + j) for j in range(b)]
        top = jnp.where(inside, jnp.where(lane - k * b == sub, 1.0, 0.0), ahead)
        for p in range(b):
            scale = 1.0 / row_of(cols[p], p)
            is_p = sub == p
            t = row_of(top, p) * scale
            top = jnp.where(is_p, t, top - cols[p] * t)
            for j in range(p + 1, b):
                t = row_of(cols[j], p) * scale
                cols[j] = jnp.where(is_p, t, cols[j] - cols[p] * t)
        following = None
        if k + 1 < count:
            old = blocks[k + 1]
            following = jnp.where(inside, 0.0, old)
            for j in range(b):
                following = following - col_of(old, k * b + j) * row_of(top, j)
        parts = [top]
        if k:
            parts.insert(0, jnp.zeros((k * b, M), F32))
        if k + 1 < count:
            parts.append(jnp.zeros((M - (k + 1) * b, M), F32))
        update = mm(jnp.concatenate(blocks, 0), jnp.concatenate(parts, 0))
        new = []
        for i in range(count):
            if i == k:
                new.append(top)
            elif i == k + 1:
                new.append(following)
            else:
                new.append(jnp.where(inside, 0.0, blocks[i]) - update[i * b : (i + 1) * b])
        blocks, ahead = new, following
    return jnp.concatenate(blocks, 0)


def tree_sum(terms):
    while len(terms) > 1:
        terms = [sum(terms[i : i + 2][1:], terms[i]) for i in range(0, len(terms), 2)]
    return terms[0]


def kernel(
    prior_hbm, kernel_hbm, off_hbm, noise_hbm, bg_hbm, obs_hbm,
    ana_ref, post_ref,
    off_ref, vec, kpad, hall, pv,
    s_src, s_rs, z_src, z_rs, s_fin, m_src, m_rs, g_src, g_rs, g_sl, g_col, g_row,
    load_sem,
    s_send, s_recv, z_send, z_recv, f_send, f_recv, m_send, m_recv,
    gs_send, gs_recv, gc_send, gc_recv, gr_send, gr_recv, sb_send, sb_recv,
):
    r = lax.axis_index("row")
    c = lax.axis_index("col")
    z = c // 4
    y_hi = (c // 2) % 2
    core = c % 2
    q = r * 2 + y_hi
    p = q * 2 + core
    owner = core == y_hi

    def plane(i):
        return (i // 4, z * 4 + i % 4)

    def summer(tile):
        return (tile // 2, z * 4 + (tile % 2) * 3)

    def send(source, target, send_sem, recv_sem, device):
        pltpu.make_async_remote_copy(
            source, target, send_sem, recv_sem, device_id=device, device_id_type=MESH
        ).start()

    def total(buffer, count, send_sem, recv_sem):
        view = buffer.at[pl.ds(0, count)]
        return pltpu.make_async_remote_copy(
            view, view, send_sem, recv_sem, device_id=(r, c), device_id_type=MESH
        )

    barrier = pltpu.get_barrier_semaphore()

    off_copy = pltpu.make_async_copy(off_hbm, off_ref, load_sem.at[0])
    off_copy.start()
    for k in range(16):
        pltpu.make_async_copy(
            kernel_hbm.at[:, pl.ds(k * 128, 128)], kpad.at[LOW + k, pl.ds(0, 128)], load_sem.at[1]
        ).start()
    prior_copy = pltpu.make_async_copy(prior_hbm, pv, load_sem.at[2])
    prior_copy.start()
    vec_copies = [
        pltpu.make_async_copy(source, vec.at[i], load_sem.at[3 + i])
        for i, source in enumerate((noise_hbm, bg_hbm, obs_hbm))
    ]
    for copy in vec_copies:
        copy.start()

    @pl.loop(1, 32)
    def _(i):
        pl.semaphore_signal(barrier, inc=1, device_id=plane((p + i) % 32), device_id_type=MESH)
        pl.semaphore_signal(barrier, inc=1, device_id=(r, (c + i) % 32), device_id_type=MESH)

    zeros = jnp.zeros((STRIDE, 128), F32)
    for start, stop in ((0, LOW), (LOW + 16, CHUNKS)):
        @pl.loop(start, stop)
        def _(i):
            kpad[i] = zeros

    off_copy.wait()
    data = kpad.at[pl.ds(LOW, 16), pl.ds(0, 128)]
    pltpu.make_async_copy(data, data, load_sem.at[1]).wait()

    lane = lax.broadcasted_iota(jnp.int32, (8, 128), 1)
    sub = lax.broadcasted_iota(jnp.int32, (8, 128), 0)
    flat = kpad.reshape(CHUNKS * STRIDE, 128)

    def build(group, carry):
        built = []
        for u in range(GROUP):
            m = group * GROUP + u
            off = off_ref[m]
            chunk = lax.shift_right_logical(off, 7)
            turn = lax.bitwise_and(off, 127)
            at_r = (LOW + 4 * r - chunk) * STRIDE + m
            at_c = (LOW + c - chunk) * STRIDE + m
            now = jnp.where(
                sub < 4, flat[pl.ds(at_r, 8, stride=STRIDE), :], flat[pl.ds(at_c, 8, stride=0), :]
            )
            before = jnp.where(
                sub < 4,
                flat[pl.ds(at_r - STRIDE, 8, stride=STRIDE), :],
                flat[pl.ds(at_c - STRIDE, 8, stride=0), :],
            )
            turned = pltpu.roll(jnp.where(lane >= 128 - turn, before, now), turn, axis=1)
            built.append((m, turned))
        for m, turned in built:
            hall[pl.ds(m, 8, stride=STRIDE), :] = turned
        return carry

    lax.fori_loop(0, M // GROUP, build, 0)

    prior_copy.wait()
    part = mm(hall[0:128, :], pv[0:128, :])
    for j in range(1, 4):
        part += mm(hall[j * STRIDE : j * STRIDE + 128, :], pv[j * 128 : (j + 1) * 128, :])
    h_c = hall[4 * STRIDE : 4 * STRIDE + 128, :]
    s_src[...] = mm_nt(h_c, part).reshape(16, 8, 128)

    pl.semaphore_wait(barrier, 62)

    @pl.loop(1, 16)
    def _(i):
        to = (q + i) % 16
        send(s_src.at[to], s_rs.at[p], s_send, s_recv, summer(to))

    @pl.when(owner)
    def _():
        s_rs[p] = s_src[q]

    @pl.when(jnp.logical_not(owner))
    def _():
        send(s_src.at[q], s_rs.at[p], s_send, s_recv, summer(q))

    g_src[...] = jnp.transpose(part).reshape(8, 16, 128)
    g_rs[r] = g_src[r]

    @pl.loop(1, 8)
    def _(i):
        to = (r + i) % 8
        send(g_src.at[to], g_rs.at[r], gs_send, gs_recv, (to, c))

    for copy in vec_copies:
        copy.wait()
    mean = mm_nt(jnp.broadcast_to(vec[1], (8, 128)), h_c)[0:1, :]
    m_src[0] = mean
    m_rs[c] = mean

    @pl.loop(1, 32)
    def _(i):
        send(m_src.at[0], m_rs.at[c], m_send, m_recv, (r, (c + i) % 32))

    @pl.when(owner)
    def _():
        total(s_rs, 31, s_send, s_recv).wait_recv()
        tile = tree_sum([s_rs[i] for i in range(32)])
        z_src[0] = tile
        z_rs[z] = tile

        @pl.loop(1, 8)
        def _(i):
            send(z_src.at[0], z_rs.at[z], z_send, z_recv, (r, (c + 4 * i) % 32))

    total(g_rs, 7, gs_send, gs_recv).wait_recv()
    g_sl[0] = tree_sum([g_rs[i] for i in range(8)])
    slot = core * 16 + y_hi * 8 + r

    @pl.loop(1, 16)
    def _(i):
        to = (z * 2 + y_hi + i) % 16
        send(g_sl.at[0], g_row.at[slot], gr_send, gr_recv, (z, (to // 2) * 4 + (to % 2) * 2 + core))

    @pl.when(z == r)
    def _():
        pltpu.make_async_copy(g_sl.at[0], g_row.at[slot], gr_recv).start()

    @pl.when(z != r)
    def _():
        send(g_sl.at[0], g_row.at[slot], gr_send, gr_recv, (z, c))

    g_col[r] = g_sl[0]

    @pl.loop(1, 8)
    def _(i):
        send(g_sl.at[0], g_col.at[r], gc_send, gc_recv, ((r + i) % 8, c))

    @pl.when(owner)
    def _():
        total(z_rs, 7, z_send, z_recv).wait_recv()
        tile = tree_sum([z_rs[i] for i in range(8)])
        z_src[1] = tile
        s_fin[q] = tile

        @pl.loop(1, 32)
        def _(i):
            send(z_src.at[1], s_fin.at[q], f_send, f_recv, plane((p + i) % 32))

    total(g_row, 16, gr_send, gr_recv).wait_recv()
    half = g_row.at[pl.ds(core * 16, 16)]
    share = pltpu.make_async_remote_copy(
        half, half, sb_send, sb_recv, device_id=(r, c + 1 - 2 * core), device_id_type=MESH
    )
    share.start()

    @pl.when(owner)
    def _():
        total(s_fin, 15, f_send, f_recv).wait_recv()

    @pl.when(jnp.logical_not(owner))
    def _():
        total(s_fin, 16, f_send, f_recv).wait_recv()

    rows = lax.broadcasted_iota(jnp.int32, (128, 128), 0)
    lanes = lax.broadcasted_iota(jnp.int32, (128, 128), 1)
    noise = jnp.where(rows == lanes, jnp.broadcast_to(vec[0], (128, 128)), 0.0)
    s_all = s_fin[...].reshape(128, 128) + noise
    inverse = spd_inverse([s_all[i * PIVOTS : (i + 1) * PIVOTS] for i in range(M // PIVOTS)], PIVOTS)

    total(g_col, 7, gc_send, gc_recv).wait_recv()
    solved = mm(g_col[...].reshape(128, 128), inverse)

    share.wait_recv()
    for j in range(4):
        first = (j % 2) * 16 + (j // 2) * 8
        g_j = g_row[first : first + 8].reshape(128, 128)
        here = slice(j * 128, (j + 1) * 128)
        post_ref[here, :] = pv[here, :] - mm_nt(g_j, solved)

    total(m_rs, 31, m_send, m_recv).wait_recv()
    mean = tree_sum([m_rs[i] for i in range(32)])
    innovation = jnp.broadcast_to(vec[2] - mean, (8, 128))
    ana_ref[...] = vec[1] + mm_nt(innovation, solved)[0:1, :]

    @pl.when(owner)
    def _():
        total(s_rs, 15, s_send, s_recv).wait_send()
        total(z_rs, 7, z_send, z_recv).wait_send()
        total(s_rs, 31, f_send, f_recv).wait_send()

    @pl.when(jnp.logical_not(owner))
    def _():
        total(s_rs, 16, s_send, s_recv).wait_send()

    total(m_rs, 31, m_send, m_recv).wait_send()
    total(g_rs, 7, gs_send, gs_recv).wait_send()
    total(g_col, 7, gc_send, gc_recv).wait_send()
    share.wait_send()

    @pl.when(z == r)
    def _():
        total(g_row, 15, gr_send, gr_recv).wait_send()

    @pl.when(z != r)
    def _():
        total(g_row, 16, gr_send, gr_recv).wait_send()


def on_device(prior_cov, kern, offsets, obs_noise, background, observed):
    vmem = pl.BlockSpec(memory_space=pltpu.VMEM)
    hbm = pl.BlockSpec(memory_space=pltpu.HBM)
    dma = pltpu.SemaphoreType.DMA

    def tiles(count, rows=8):
        return pltpu.VMEM((count, rows, 128), F32)

    ana, post = pl.pallas_call(
        kernel,
        name="analysis",
        out_shape=(jax.ShapeDtypeStruct((1, 128), F32), jax.ShapeDtypeStruct((512, 128), F32)),
        in_specs=[hbm] * 6,
        out_specs=(vmem, vmem),
        scratch_shapes=[
            pltpu.SMEM((128,), jnp.int32),
            tiles(3, 1),
            tiles(CHUNKS, STRIDE),
            pltpu.VMEM((8 * STRIDE, 128), F32),
            pltpu.VMEM((512, 128), F32),
            tiles(16), tiles(32), tiles(2), tiles(8), tiles(16),
            tiles(1, 1), tiles(32, 1),
            tiles(8, 16), tiles(8, 16), tiles(1, 16), tiles(8, 16), tiles(32, 16),
            dma((6,)),
        ]
        + [dma] * 16,
        compiler_params=pltpu.CompilerParams(
            collective_id=0, has_side_effects=True, vmem_limit_bytes=66519040
        ),
    )(
        prior_cov,
        kern,
        offsets,
        obs_noise.reshape(1, 128),
        background.reshape(1, 128),
        observed.reshape(1, 128),
    )
    return ana.reshape(128), post


def solution(mesh):
    placed = (P("row", "col"), P(), P(), P(), P("col"), P())
    return jax.shard_map(
        on_device,
        mesh=mesh,
        in_specs=placed,
        out_specs=(P("col"), P("row", "col")),
        check_vma=False,
    )
```

time: 41.2 us -> 33.7 us (0.82)
  the two profiles are of different devices: /device:TPU:3 before, /device:TPU:1 now
where the time goes in v2:
time: 33.7 us; the launch traced here: 33.5 us
  Pallas kernels  30.2 us (90%)
  local copies, waits for them, and re-layouts  2.74 us (8%)
  between operations  0.65 us (2%)
    pallas_call x1, Pallas kernels, on_device(): pl.pallas_call(kernel, name='analysis', out_shape=(jax.ShapeDtypeStruct((...  30.2 us
    unnamed x4, local copies, waits for them, and re-layouts  2.74 us

profile of v2, /device:TPU:1, one launch (start us, length us, event | category | flops | bytes accessed | tf_op | source)
XLA Modules:
  0.0 33.5 jit_solution(16314212371167684124)
XLA Ops:
  0.6 30.2 %analysis.1 = (f32[1,128]{1,0:T(1,128)}, f32[512,128]{1,0:T(8,128)}) custom-call(f32[512,128]{1,0:T(8,128)} %prior_hbm.1, f32[128,2048]{1,0:T(8,128)} %kernel_hbm.1, s32[128]{0:T(128)} %off_hbm.1, f32[1,128]{1,0:T(1,128)} %bitcast.4, f32[1,128]{1,0:T(1,128)} %bitcast.5, f32[1,128]{1,0:T(1,128)} %bitcast.6), custom_call_target="tpu_custom_call" | custom-call | tf_op jit(solution)/shard_map/analysis/pallas_call | solution.py:332
  30.8 0.0 copy-start
  30.8 0.6 %copy-done = f32[1,128]{1,0:T(1,128)S(1)} copy-done((f32[1,128]{1,0:T(1,128)S(1)}, f32[1,128]{1,0:T(1,128)}, u32[]{:S(2)}) %copy-start) | copy-done | bytes 536
  31.4 0.5 %copy.10 = f32[128]{0:T(128)} copy(f32[128]{0:T(128)S(1)} %bitcast.7) | data formatting | bytes 1024
  31.9 1.7 %copy.11 = f32[512,128]{1,0:T(8,128)} copy(f32[512,128]{1,0:T(8,128)} %get-tuple-element.9) | data formatting | bytes 524288
Async XLA Ops:
  30.8 0.6 %copy-start = (f32[1,128]{1,0:T(1,128)S(1)}, f32[1,128]{1,0:T(1,128)}, u32[]{:S(2)}) copy-start(f32[1,128]{1,0:T(1,128)} %get-tuple-element.4) | copy-start | bytes 1540

commit v3 on v2

--- a/solution.py
+++ b/solution.py
@@ -82,9 +82,9 @@
 
 def kernel(
     prior_hbm, kernel_hbm, off_hbm, noise_hbm, bg_hbm, obs_hbm,
-    ana_ref, post_ref,
-    off_ref, vec, kpad, hall, pv,
-    s_src, s_rs, z_src, z_rs, s_fin, m_src, m_rs, g_src, g_rs, g_sl, g_col, g_row,
+    solved_ref, innovation_ref, pv, g_row,
+    off_ref, vec, kpad, hall,
+    s_src, s_rs, z_src, z_rs, s_fin, m_src, m_rs, g_src, g_rs, g_sl, g_col,
     load_sem,
     s_send, s_recv, z_send, z_recv, f_send, f_recv, m_send, m_recv,
     gs_send, gs_recv, gc_send, gc_recv, gr_send, gr_recv, sb_send, sb_recv,
@@ -282,43 +282,57 @@
     s_all = s_fin[...].reshape(128, 128) + noise
     inverse = spd_inverse([s_all[i * PIVOTS : (i + 1) * PIVOTS] for i in range(M // PIVOTS)], PIVOTS)
 
+    total(m_rs, 31, m_send, m_recv).wait_recv()
+    mean = tree_sum([m_rs[i] for i in range(32)])
+    innovation_ref[...] = jnp.broadcast_to(vec[2] - mean, (8, 128))
+
     total(g_col, 7, gc_send, gc_recv).wait_recv()
-    solved = mm(g_col[...].reshape(128, 128), inverse)
+    solved_ref[...] = mm(g_col[...].reshape(128, 128), inverse)
 
     share.wait_recv()
+
+    @pl.when(owner)
+    def _():
+        total(s_rs, 15, s_send, s_recv).wait_send()
+        total(z_rs, 7, z_send, z_recv).wait_send()
+        total(s_rs, 31, f_send, f_recv).wait_send()
+
+    @pl.when(jnp.logical_not(owner))
+    def _():
+        total(s_rs, 16, s_send, s_recv).wait_send()
+
+    total(m_rs, 31, m_send, m_recv).wait_send()
+    total(g_rs, 7, gs_send, gs_recv).wait_send()
+    total(g_col, 7, gc_send, gc_recv).wait_send()
+    share.wait_send()
+
+    @pl.when(z == r)
+    def _():
+        total(g_row, 15, gr_send, gr_recv).wait_send()
+
+    @pl.when(z != r)
+    def _():
+        total(g_row, 16, gr_send, gr_recv).wait_send()
+
+
+def finish(solved_ref, innovation_ref, pv, g_row, bg_hbm, ana_hbm, post_hbm, bg, ana, post, sem):
+    bg_copy = pltpu.make_async_copy(bg_hbm, bg, sem.at[0])
+    bg_copy.start()
+    solved = solved_ref[...]
+    copies = []
     for j in range(4):
         first = (j % 2) * 16 + (j // 2) * 8
         g_j = g_row[first : first + 8].reshape(128, 128)
         here = slice(j * 128, (j + 1) * 128)
-        post_ref[here, :] = pv[here, :] - mm_nt(g_j, solved)
-
-    total(m_rs, 31, m_send, m_recv).wait_recv()
-    mean = tree_sum([m_rs[i] for i in range(32)])
-    innovation = jnp.broadcast_to(vec[2] - mean, (8, 128))
-    ana_ref[...] = vec[1] + mm_nt(innovation, solved)[0:1, :]
-
-    @pl.when(owner)
-    def _():
-        total(s_rs, 15, s_send, s_recv).wait_send()
-        total(z_rs, 7, z_send, z_recv).wait_send()
-        total(s_rs, 31, f_send, f_recv).wait_send()
-
-    @pl.when(jnp.logical_not(owner))
-    def _():
-        total(s_rs, 16, s_send, s_recv).wait_send()
-
-    total(m_rs, 31, m_send, m_recv).wait_send()
-    total(g_rs, 7, gs_send, gs_recv).wait_send()
-    total(g_col, 7, gc_send, gc_recv).wait_send()
-    share.wait_send()
-
-    @pl.when(z == r)
-    def _():
-        total(g_row, 15, gr_send, gr_recv).wait_send()
-
-    @pl.when(z != r)
-    def _():
-        total(g_row, 16, gr_send, gr_recv).wait_send()
+        post[here, :] = pv[here, :] - mm_nt(g_j, solved)
+        copies.append(pltpu.make_async_copy(post.at[here], post_hbm.at[here], sem.at[1 + j]))
+        copies[-1].start()
+    bg_copy.wait()
+    ana[...] = bg[...] + mm_nt(innovation_ref[...], solved)[0:1, :]
+    copies.append(pltpu.make_async_copy(ana, ana_hbm, sem.at[5]))
+    copies[-1].start()
+    for copy in copies:
+        copy.wait()
 
 
 def on_device(prior_cov, kern, offsets, obs_noise, background, observed):
@@ -329,35 +343,52 @@
     def tiles(count, rows=8):
         return pltpu.VMEM((count, rows, 128), F32)
 
-    ana, post = pl.pallas_call(
+    def array(*shape):
+        return jax.ShapeDtypeStruct(shape, F32)
+
+    operands = [
+        pltpu.with_memory_space_constraint(x, pltpu.HBM)
+        for x in (
+            prior_cov,
+            kern,
+            offsets,
+            obs_noise.reshape(1, 128),
+            background.reshape(1, 128),
+            observed.reshape(1, 128),
+        )
+    ]
+    solved, innovation, prior_copy, pieces = pl.pallas_call(
         kernel,
         name="analysis",
-        out_shape=(jax.ShapeDtypeStruct((1, 128), F32), jax.ShapeDtypeStruct((512, 128), F32)),
+        out_shape=(array(128, 128), array(8, 128), array(512, 128), array(32, 16, 128)),
         in_specs=[hbm] * 6,
-        out_specs=(vmem, vmem),
+        out_specs=(vmem,) * 4,
         scratch_shapes=[
             pltpu.SMEM((128,), jnp.int32),
             tiles(3, 1),
             tiles(CHUNKS, STRIDE),
             pltpu.VMEM((8 * STRIDE, 128), F32),
-            pltpu.VMEM((512, 128), F32),
             tiles(16), tiles(32), tiles(2), tiles(8), tiles(16),
             tiles(1, 1), tiles(32, 1),
-            tiles(8, 16), tiles(8, 16), tiles(1, 16), tiles(8, 16), tiles(32, 16),
+            tiles(8, 16), tiles(8, 16), tiles(1, 16), tiles(8, 16),
             dma((6,)),
         ]
         + [dma] * 16,
         compiler_params=pltpu.CompilerParams(
-            collective_id=0, has_side_effects=True, vmem_limit_bytes=66519040
+            collective_id=0, has_side_effects=True, vmem_limit_bytes=40 * 1024 * 1024
         ),
-    )(
-        prior_cov,
-        kern,
-        offsets,
-        obs_noise.reshape(1, 128),
-        background.reshape(1, 128),
-        observed.reshape(1, 128),
-    )
+    )(*operands)
+    ana, post = pl.pallas_call(
+        finish,
+        name="finish",
+        out_shape=(array(1, 128), array(512, 128)),
+        in_specs=[vmem] * 4 + [hbm],
+        out_specs=(hbm, hbm),
+        scratch_shapes=[
+            pltpu.VMEM((1, 128), F32), pltpu.VMEM((1, 128), F32), pltpu.VMEM((512, 128), F32), dma((6,)),
+        ],
+        compiler_params=pltpu.CompilerParams(vmem_limit_bytes=40 * 1024 * 1024),
+    )(solved, innovation, prior_copy, pieces, operands[4])
     return ana.reshape(128), post
 
 

time: 33.7 us -> 31 us (0.920)
  local copies, waits for them, and re-layouts: 2.74 us -> 0 us
    unnamed x4 -> x0, local copies, waits for them, and re-layouts: 2.74 us -> none
    pallas_call x1 -> x2, Pallas kernels: 30.2 us -> 30.3 us  [the longest x1 28.6 us: on_device(): pl.pallas_call(kernel, name='analysis', out_shape=(array(128, 128), array...]
where the time goes in v3:
time: 31 us; the launch traced here: 30.9 us
  Pallas kernels  30.3 us (98%)
  between operations  0.64 us (2%)
    pallas_call x1, Pallas kernels, on_device(): pl.pallas_call(kernel, name='analysis', out_shape=(array(128, 128), array...  28.6 us
    pallas_call x1, Pallas kernels, on_device(): pl.pallas_call(finish, name='finish', out_shape=(array(1, 128), array(512...  1.75 us

profile of v3, /device:TPU:1, one launch (start us, length us, event | category | flops | bytes accessed | tf_op | source)
XLA Modules:
  0.0 30.9 jit_solution(9364100856296391369)
XLA Ops:
  0.6 28.6 %analysis.1 = (f32[128,128]{1,0:T(8,128)S(1)}, f32[8,128]{1,0:T(8,128)S(1)}, f32[512,128]{1,0:T(8,128)S(1)}, f32[32,16,128]{2,1,0:T(8,128)S(1)}) custom-call(f32[512,128]{1,0:T(8,128)} %prior_hbm.1, f32[128,2048]{1,0:T(8,128)} %kernel_hbm.1, s32[128]{0:T(128)} %off_hbm.1, f32[1,128]{1,0:T(1,128)} %bitcast.6, f32[1,128]{1,0:T(1,128)} %bitcast.4, f32[1,128]{1,0:T(1,128)} %bitcast.7), custom_call_target="tpu_custom_call" | custom-call | tf_op jit(solution)/shard_map/analysis/pallas_call | solution.py:360
  29.2 1.7 %finish.1 = (f32[1,128]{1,0:T(1,128)}, f32[512,128]{1,0:T(8,128)}) custom-call(f32[128,128]{1,0:T(8,128)S(1)} %get-tuple-element.8.solved_ref, f32[8,128]{1,0:T(8,128)S(1)} %get-tuple-element.9.innovation_ref, f32[512,128]{1,0:T(8,128)S(1)} %get-tuple-element.10.pv, f32[32,16,128]{2,1,0:T(8,128)S(1)} %get-tuple-element.11.g_row, f32[1,128]{1,0:T(1,128)} %bitcast.5), custom_call_target="tpu_custom_call" | custom-call | tf_op jit(solution)/shard_map/finish/pallas_call | solution.py:381

commit v4 on v3

--- a/solution.py
+++ b/solution.py
@@ -11,7 +11,18 @@
 LOW = 24
 CHUNKS = 64
 STRIDE = 136
-GROUP = 32
+GROUP = 64
+GAP = GROUP + 8
+
+
+def ring(d, n):
+    return min(d, n - d)
+
+
+PLANE_STEPS = sorted(
+    ((dx, dy) for dx in range(4) for dy in range(4) if dx or dy), key=lambda d: -ring(d[0], 4) - ring(d[1], 4)
+)
+PLANES_STEPS = sorted(range(1, 8), key=lambda d: -ring(d, 8))
 PIVOTS = 16
 
 
@@ -83,10 +94,10 @@
 def kernel(
     prior_hbm, kernel_hbm, off_hbm, noise_hbm, bg_hbm, obs_hbm,
     solved_ref, innovation_ref, pv, g_row,
-    off_ref, vec, kpad, hall,
-    s_src, s_rs, z_src, z_rs, s_fin, m_src, m_rs, g_src, g_rs, g_sl, g_col,
-    load_sem,
-    s_send, s_recv, z_send, z_recv, f_send, f_recv, m_send, m_recv,
+    off_ref, vec, kpad_0, kpad_1, hall,
+    s_src, s_rs, z_src, z_rs, s_fin, m_src, m_rs, m_all, g_src, g_rs, g_sl, g_col,
+    load_sem, group_sem, ready,
+    s_send, s_recv, z_send, z_recv, f_send, f_recv, m_send, m_recv, ma_send, ma_recv,
     gs_send, gs_recv, gc_send, gc_recv, gr_send, gr_recv, sb_send, sb_recv,
 ):
     r = lax.axis_index("row")
@@ -98,11 +109,15 @@
     p = q * 2 + core
     owner = core == y_hi
 
+    x = r // 2
+    y = y_hi * 2 + r % 2
+
+    def chip(dx, dy):
+        to_x, to_y = (x + dx) % 4, (y + dy) % 4
+        return to_x * 2 + to_y % 2, to_y // 2
+
     def plane(i):
         return (i // 4, z * 4 + i % 4)
-
-    def summer(tile):
-        return (tile // 2, z * 4 + (tile % 2) * 3)
 
     def send(source, target, send_sem, recv_sem, device):
         pltpu.make_async_remote_copy(
@@ -117,12 +132,26 @@
 
     barrier = pltpu.get_barrier_semaphore()
 
+    def greet(device):
+        pl.semaphore_signal(barrier, inc=1, device_id=device, device_id_type=MESH)
+
+    for dx, dy in PLANE_STEPS:
+        row, half = chip(dx, dy)
+        greet((row, z * 4 + half * 2))
+        greet((row, z * 4 + half * 2 + 1))
+    for dz in PLANES_STEPS:
+        greet((r, (c + 4 * dz) % 32))
+    greet((r, c + 1 - 2 * core))
+
     off_copy = pltpu.make_async_copy(off_hbm, off_ref, load_sem.at[0])
     off_copy.start()
-    for k in range(16):
-        pltpu.make_async_copy(
-            kernel_hbm.at[:, pl.ds(k * 128, 128)], kpad.at[LOW + k, pl.ds(0, 128)], load_sem.at[1]
-        ).start()
+    kpads = (kpad_0, kpad_1)
+    for group in range(M // GROUP):
+        rows = pl.ds(group * GROUP, GROUP)
+        for k in range(16):
+            pltpu.make_async_copy(
+                kernel_hbm.at[rows, pl.ds(k * 128, 128)], kpads[group].at[LOW + k, pl.ds(0, GROUP)], group_sem.at[group]
+            ).start()
     prior_copy = pltpu.make_async_copy(prior_hbm, pv, load_sem.at[2])
     prior_copy.start()
     vec_copies = [
@@ -132,63 +161,55 @@
     for copy in vec_copies:
         copy.start()
 
-    @pl.loop(1, 32)
-    def _(i):
-        pl.semaphore_signal(barrier, inc=1, device_id=plane((p + i) % 32), device_id_type=MESH)
-        pl.semaphore_signal(barrier, inc=1, device_id=(r, (c + i) % 32), device_id_type=MESH)
-
-    zeros = jnp.zeros((STRIDE, 128), F32)
-    for start, stop in ((0, LOW), (LOW + 16, CHUNKS)):
+    zeros = jnp.zeros((GROUP, 128), F32)
+    for start, stop in ((LOW - 17, LOW), (LOW + 16, LOW + 32)):
         @pl.loop(start, stop)
         def _(i):
-            kpad[i] = zeros
+            for kpad in kpads:
+                kpad[i, 0:GROUP] = zeros
 
     off_copy.wait()
-    data = kpad.at[pl.ds(LOW, 16), pl.ds(0, 128)]
-    pltpu.make_async_copy(data, data, load_sem.at[1]).wait()
 
     lane = lax.broadcasted_iota(jnp.int32, (8, 128), 1)
     sub = lax.broadcasted_iota(jnp.int32, (8, 128), 0)
-    flat = kpad.reshape(CHUNKS * STRIDE, 128)
-
-    def build(group, carry):
+
+    for group in range(M // GROUP):
+        data = kpads[group].at[pl.ds(LOW, 16), pl.ds(0, GROUP)]
+        flat = kpads[group].reshape(CHUNKS * GAP, 128)
+        pltpu.make_async_copy(data, data, group_sem.at[group]).wait()
         built = []
         for u in range(GROUP):
             m = group * GROUP + u
             off = off_ref[m]
             chunk = lax.shift_right_logical(off, 7)
             turn = lax.bitwise_and(off, 127)
-            at_r = (LOW + 4 * r - chunk) * STRIDE + m
-            at_c = (LOW + c - chunk) * STRIDE + m
+            at_r = (LOW + 4 * r - chunk) * GAP + u
+            at_c = (LOW + c - chunk) * GAP + u
             now = jnp.where(
-                sub < 4, flat[pl.ds(at_r, 8, stride=STRIDE), :], flat[pl.ds(at_c, 8, stride=0), :]
+                sub < 4, flat[pl.ds(at_r, 8, stride=GAP), :], flat[pl.ds(at_c, 8, stride=0), :]
             )
             before = jnp.where(
                 sub < 4,
-                flat[pl.ds(at_r - STRIDE, 8, stride=STRIDE), :],
-                flat[pl.ds(at_c - STRIDE, 8, stride=0), :],
+                flat[pl.ds(at_r - GAP, 8, stride=GAP), :],
+                flat[pl.ds(at_c - GAP, 8, stride=0), :],
             )
             turned = pltpu.roll(jnp.where(lane >= 128 - turn, before, now), turn, axis=1)
             built.append((m, turned))
         for m, turned in built:
             hall[pl.ds(m, 8, stride=STRIDE), :] = turned
-        return carry
-
-    lax.fori_loop(0, M // GROUP, build, 0)
 
     prior_copy.wait()
-    part = mm(hall[0:128, :], pv[0:128, :])
-    for j in range(1, 4):
-        part += mm(hall[j * STRIDE : j * STRIDE + 128, :], pv[j * 128 : (j + 1) * 128, :])
+    h_r = jnp.concatenate([hall[j * STRIDE : j * STRIDE + 128, :] for j in range(4)], 1)
+    part = mm(h_r, pv[...])
     h_c = hall[4 * STRIDE : 4 * STRIDE + 128, :]
     s_src[...] = mm_nt(h_c, part).reshape(16, 8, 128)
 
-    pl.semaphore_wait(barrier, 62)
-
-    @pl.loop(1, 16)
-    def _(i):
-        to = (q + i) % 16
-        send(s_src.at[to], s_rs.at[p], s_send, s_recv, summer(to))
+    pl.semaphore_wait(barrier, 38)
+
+    for dx, dy in PLANE_STEPS:
+        row, half = chip(dx, dy)
+        to = row * 2 + half
+        send(s_src.at[to], s_rs.at[p], s_send, s_recv, (row, z * 4 + half * 3))
 
     @pl.when(owner)
     def _():
@@ -196,7 +217,7 @@
 
     @pl.when(jnp.logical_not(owner))
     def _():
-        send(s_src.at[q], s_rs.at[p], s_send, s_recv, summer(q))
+        send(s_src.at[q], s_rs.at[p], s_send, s_recv, (r, z * 4 + y_hi * 3))
 
     g_src[...] = jnp.transpose(part).reshape(8, 16, 128)
     g_rs[r] = g_src[r]
@@ -210,11 +231,17 @@
         copy.wait()
     mean = mm_nt(jnp.broadcast_to(vec[1], (8, 128)), h_c)[0:1, :]
     m_src[0] = mean
-    m_rs[c] = mean
-
-    @pl.loop(1, 32)
-    def _(i):
-        send(m_src.at[0], m_rs.at[c], m_send, m_recv, (r, (c + i) % 32))
+    m_rs[z] = mean
+
+    @pl.loop(1, 8)
+    def _(i):
+        send(m_src.at[0], m_rs.at[z], m_send, m_recv, (r, (c + 4 * i) % 32))
+
+    @pl.loop(0, 8)
+    def _(i):
+        pl.semaphore_signal(
+            ready, inc=1, device_id=(i, z * 4 + (1 - y_hi) * 2 + core), device_id_type=MESH
+        )
 
     @pl.when(owner)
     def _():
@@ -222,13 +249,14 @@
         tile = tree_sum([s_rs[i] for i in range(32)])
         z_src[0] = tile
         z_rs[z] = tile
-
-        @pl.loop(1, 8)
-        def _(i):
-            send(z_src.at[0], z_rs.at[z], z_send, z_recv, (r, (c + 4 * i) % 32))
+        for dz in PLANES_STEPS:
+            send(z_src.at[0], z_rs.at[z], z_send, z_recv, (r, (c + 4 * dz) % 32))
 
     total(g_rs, 7, gs_send, gs_recv).wait_recv()
-    g_sl[0] = tree_sum([g_rs[i] for i in range(8)])
+    pl.semaphore_wait(ready, 8)
+    piece = tree_sum([g_rs[i] for i in range(8)])
+    g_sl[0] = piece
+    g_col[r] = piece
     slot = core * 16 + y_hi * 8 + r
 
     @pl.loop(1, 16)
@@ -243,8 +271,6 @@
     @pl.when(z != r)
     def _():
         send(g_sl.at[0], g_row.at[slot], gr_send, gr_recv, (z, c))
-
-    g_col[r] = g_sl[0]
 
     @pl.loop(1, 8)
     def _(i):
@@ -257,9 +283,25 @@
         z_src[1] = tile
         s_fin[q] = tile
 
-        @pl.loop(1, 32)
-        def _(i):
-            send(z_src.at[1], s_fin.at[q], f_send, f_recv, plane((p + i) % 32))
+        for dx, dy in PLANE_STEPS + [(0, 0)]:
+            row, half = chip(dx, dy)
+            for other in (0, 1):
+                if dx or dy:
+                    to = (row, z * 4 + half * 2 + other)
+                elif other:
+                    to = (r, c + 1 - 2 * core)
+                else:
+                    continue
+                send(z_src.at[1], s_fin.at[q], f_send, f_recv, to)
+
+    total(m_rs, 7, m_send, m_recv).wait_recv()
+    m_src[1] = tree_sum([m_rs[i] for i in range(8)])
+    place = y_hi * 2 + core
+    m_all[place] = m_src[1]
+
+    @pl.loop(1, 4)
+    def _(i):
+        send(m_src.at[1], m_all.at[place], ma_send, ma_recv, (r, z * 4 + (place + i) % 4))
 
     total(g_row, 16, gr_send, gr_recv).wait_recv()
     half = g_row.at[pl.ds(core * 16, 16)]
@@ -282,8 +324,8 @@
     s_all = s_fin[...].reshape(128, 128) + noise
     inverse = spd_inverse([s_all[i * PIVOTS : (i + 1) * PIVOTS] for i in range(M // PIVOTS)], PIVOTS)
 
-    total(m_rs, 31, m_send, m_recv).wait_recv()
-    mean = tree_sum([m_rs[i] for i in range(32)])
+    total(m_all, 3, ma_send, ma_recv).wait_recv()
+    mean = tree_sum([m_all[i] for i in range(4)])
     innovation_ref[...] = jnp.broadcast_to(vec[2] - mean, (8, 128))
 
     total(g_col, 7, gc_send, gc_recv).wait_recv()
@@ -301,7 +343,8 @@
     def _():
         total(s_rs, 16, s_send, s_recv).wait_send()
 
-    total(m_rs, 31, m_send, m_recv).wait_send()
+    total(m_rs, 7, m_send, m_recv).wait_send()
+    total(m_all, 3, ma_send, ma_recv).wait_send()
     total(g_rs, 7, gs_send, gs_recv).wait_send()
     total(g_col, 7, gc_send, gc_recv).wait_send()
     share.wait_send()
@@ -366,14 +409,17 @@
         scratch_shapes=[
             pltpu.SMEM((128,), jnp.int32),
             tiles(3, 1),
-            tiles(CHUNKS, STRIDE),
+            tiles(CHUNKS, GAP),
+            tiles(CHUNKS, GAP),
             pltpu.VMEM((8 * STRIDE, 128), F32),
             tiles(16), tiles(32), tiles(2), tiles(8), tiles(16),
-            tiles(1, 1), tiles(32, 1),
+            tiles(2, 1), tiles(8, 1), tiles(4, 1),
             tiles(8, 16), tiles(8, 16), tiles(1, 16), tiles(8, 16),
             dma((6,)),
+            dma((M // GROUP,)),
+            pltpu.SemaphoreType.REGULAR,
         ]
-        + [dma] * 16,
+        + [dma] * 18,
         compiler_params=pltpu.CompilerParams(
             collective_id=0, has_side_effects=True, vmem_limit_bytes=40 * 1024 * 1024
         ),

time: 31 us -> 29.9 us (0.965)
  Pallas kernels: 30.3 us -> 29.2 us
    pallas_call x1, Pallas kernels: 28.6 us -> 27.4 us  [on_device(): pl.pallas_call(kernel, name='analysis', out_shape=(array(128, 128), array...]
where the time goes in v4:
time: 29.9 us; the launch traced here: 29.8 us
  Pallas kernels  29.2 us (98%)
  between operations  0.64 us (2%)
    pallas_call x1, Pallas kernels, on_device(): pl.pallas_call(kernel, name='analysis', out_shape=(array(128, 128), array...  27.4 us
    pallas_call x1, Pallas kernels, on_device(): pl.pallas_call(finish, name='finish', out_shape=(array(1, 128), array(512...  1.75 us

profile of v4, /device:TPU:1, one launch (start us, length us, event | category | flops | bytes accessed | tf_op | source)
XLA Modules:
  0.0 29.8 jit_solution(11258566639459840106)
XLA Ops:
  0.6 27.4 %analysis.1 = (f32[128,128]{1,0:T(8,128)S(1)}, f32[8,128]{1,0:T(8,128)S(1)}, f32[512,128]{1,0:T(8,128)S(1)}, f32[32,16,128]{2,1,0:T(8,128)S(1)}) custom-call(f32[512,128]{1,0:T(8,128)} %prior_hbm.1, f32[128,2048]{1,0:T(8,128)} %kernel_hbm.1, s32[128]{0:T(128)} %off_hbm.1, f32[1,128]{1,0:T(1,128)} %bitcast.6, f32[1,128]{1,0:T(1,128)} %bitcast.4, f32[1,128]{1,0:T(1,128)} %bitcast.7), custom_call_target="tpu_custom_call" | custom-call | tf_op jit(solution)/shard_map/analysis/pallas_call | solution.py:403
  28.0 1.7 %finish.1 = (f32[1,128]{1,0:T(1,128)}, f32[512,128]{1,0:T(8,128)}) custom-call(f32[128,128]{1,0:T(8,128)S(1)} %get-tuple-element.8.solved_ref, f32[8,128]{1,0:T(8,128)S(1)} %get-tuple-element.9.innovation_ref, f32[512,128]{1,0:T(8,128)S(1)} %get-tuple-element.10.pv, f32[32,16,128]{2,1,0:T(8,128)S(1)} %get-tuple-element.11.g_row, f32[1,128]{1,0:T(1,128)} %bitcast.5), custom_call_target="tpu_custom_call" | custom-call | tf_op jit(solution)/shard_map/finish/pallas_call | solution.py:427

commit v5 on v4

--- a/solution.py
+++ b/solution.py
@@ -93,7 +93,7 @@
 
 def kernel(
     prior_hbm, kernel_hbm, off_hbm, noise_hbm, bg_hbm, obs_hbm,
-    solved_ref, innovation_ref, pv, g_row,
+    solved_ref, vectors_ref, pv, g_row,
     off_ref, vec, kpad_0, kpad_1, hall,
     s_src, s_rs, z_src, z_rs, s_fin, m_src, m_rs, m_all, g_src, g_rs, g_sl, g_col,
     load_sem, group_sem, ready,
@@ -135,13 +135,15 @@
     def greet(device):
         pl.semaphore_signal(barrier, inc=1, device_id=device, device_id_type=MESH)
 
+    greetings = [(ring(dz, 8) + 0.5, (r, (c + 4 * dz) % 32)) for dz in range(1, 8)]
     for dx, dy in PLANE_STEPS:
         row, half = chip(dx, dy)
-        greet((row, z * 4 + half * 2))
-        greet((row, z * 4 + half * 2 + 1))
-    for dz in PLANES_STEPS:
-        greet((r, (c + 4 * dz) % 32))
-    greet((r, c + 1 - 2 * core))
+        for other in (0, 1):
+            greetings.append((ring(dx, 4) + ring(dy, 4), (row, z * 4 + half * 2 + other)))
+    greetings.sort(key=lambda g: -g[0])
+    greetings = [device for _, device in greetings] + [(r, c + 1 - 2 * core)]
+    for device in greetings[:16]:
+        greet(device)
 
     off_copy = pltpu.make_async_copy(off_hbm, off_ref, load_sem.at[0])
     off_copy.start()
@@ -152,6 +154,9 @@
             pltpu.make_async_copy(
                 kernel_hbm.at[rows, pl.ds(k * 128, 128)], kpads[group].at[LOW + k, pl.ds(0, GROUP)], group_sem.at[group]
             ).start()
+        if group == 0:
+            for device in greetings[16:]:
+                greet(device)
     prior_copy = pltpu.make_async_copy(prior_hbm, pv, load_sem.at[2])
     prior_copy.start()
     vec_copies = [
@@ -326,7 +331,8 @@
 
     total(m_all, 3, ma_send, ma_recv).wait_recv()
     mean = tree_sum([m_all[i] for i in range(4)])
-    innovation_ref[...] = jnp.broadcast_to(vec[2] - mean, (8, 128))
+    vectors_ref[0] = jnp.broadcast_to(vec[2] - mean, (8, 128))
+    vectors_ref[1] = jnp.broadcast_to(vec[1], (8, 128))
 
     total(g_col, 7, gc_send, gc_recv).wait_recv()
     solved_ref[...] = mm(g_col[...].reshape(128, 128), inverse)
@@ -358,22 +364,18 @@
         total(g_row, 16, gr_send, gr_recv).wait_send()
 
 
-def finish(solved_ref, innovation_ref, pv, g_row, bg_hbm, ana_hbm, post_hbm, bg, ana, post, sem):
-    bg_copy = pltpu.make_async_copy(bg_hbm, bg, sem.at[0])
-    bg_copy.start()
+def finish(solved_ref, vectors_ref, pv, g_row, ana_hbm, post_hbm, ana, post, sem):
     solved = solved_ref[...]
-    copies = []
+    ana[...] = (vectors_ref[1] + mm_nt(vectors_ref[0], solved))[0:1, :]
+    copies = [pltpu.make_async_copy(ana, ana_hbm, sem.at[4])]
+    copies[0].start()
     for j in range(4):
         first = (j % 2) * 16 + (j // 2) * 8
         g_j = g_row[first : first + 8].reshape(128, 128)
         here = slice(j * 128, (j + 1) * 128)
         post[here, :] = pv[here, :] - mm_nt(g_j, solved)
-        copies.append(pltpu.make_async_copy(post.at[here], post_hbm.at[here], sem.at[1 + j]))
+        copies.append(pltpu.make_async_copy(post.at[here], post_hbm.at[here], sem.at[j]))
         copies[-1].start()
-    bg_copy.wait()
-    ana[...] = bg[...] + mm_nt(innovation_ref[...], solved)[0:1, :]
-    copies.append(pltpu.make_async_copy(ana, ana_hbm, sem.at[5]))
-    copies[-1].start()
     for copy in copies:
         copy.wait()
 
@@ -400,10 +402,10 @@
             observed.reshape(1, 128),
         )
     ]
-    solved, innovation, prior_copy, pieces = pl.pallas_call(
+    solved, vectors, prior_copy, pieces = pl.pallas_call(
         kernel,
         name="analysis",
-        out_shape=(array(128, 128), array(8, 128), array(512, 128), array(32, 16, 128)),
+        out_shape=(array(128, 128), array(2, 8, 128), array(512, 128), array(32, 16, 128)),
         in_specs=[hbm] * 6,
         out_specs=(vmem,) * 4,
         scratch_shapes=[
@@ -428,13 +430,13 @@
         finish,
         name="finish",
         out_shape=(array(1, 128), array(512, 128)),
-        in_specs=[vmem] * 4 + [hbm],
+        in_specs=[vmem] * 4,
         out_specs=(hbm, hbm),
         scratch_shapes=[
-            pltpu.VMEM((1, 128), F32), pltpu.VMEM((1, 128), F32), pltpu.VMEM((512, 128), F32), dma((6,)),
+            pltpu.VMEM((1, 128), F32), pltpu.VMEM((512, 128), F32), dma((5,)),
         ],
         compiler_params=pltpu.CompilerParams(vmem_limit_bytes=40 * 1024 * 1024),
-    )(solved, innovation, prior_copy, pieces, operands[4])
+    )(solved, vectors, prior_copy, pieces)
     return ana.reshape(128), post
 
 

time: 29.9 us -> 29.9 us (level)
    pallas_call x1, Pallas kernels: 1.75 us -> 1.44 us  [on_device(): pl.pallas_call(finish, name='finish', out_shape=(array(1, 128), array(512...]
where the time goes in v5:
time: 29.9 us; the launch traced here: 29.8 us
  Pallas kernels  29.1 us (97%)
  between operations  0.64 us (2%)
    pallas_call x1, Pallas kernels, on_device(): pl.pallas_call(kernel, name='analysis', out_shape=(array(128, 128), array...  27.7 us
    pallas_call x1, Pallas kernels, on_device(): pl.pallas_call(finish, name='finish', out_shape=(array(1, 128), array(512...  1.44 us

profile of v5, /device:TPU:1, one launch (start us, length us, event | category | flops | bytes accessed | tf_op | source)
XLA Modules:
  0.0 29.8 jit_solution(5383934695859463308)
XLA Ops:
  0.6 27.7 %analysis.1 = (f32[128,128]{1,0:T(8,128)S(1)}, f32[2,8,128]{2,1,0:T(8,128)S(1)}, f32[512,128]{1,0:T(8,128)S(1)}, f32[32,16,128]{2,1,0:T(8,128)S(1)}) custom-call(f32[512,128]{1,0:T(8,128)} %prior_hbm.1, f32[128,2048]{1,0:T(8,128)} %kernel_hbm.1, s32[128]{0:T(128)} %off_hbm.1, f32[1,128]{1,0:T(1,128)} %bitcast.4, f32[1,128]{1,0:T(1,128)} %bitcast.5, ...), custom_call_target="tpu_custom_call" | custom-call | tf_op jit(solution)/shard_map/analysis/pallas_call | solution.py:405
  28.3 1.4 %finish.1 = (f32[1,128]{1,0:T(1,128)}, f32[512,128]{1,0:T(8,128)}) custom-call(f32[128,128]{1,0:T(8,128)S(1)} %get-tuple-element.8.solved_ref, f32[2,8,128]{2,1,0:T(8,128)S(1)} %get-tuple-element.9.vectors_ref, f32[512,128]{1,0:T(8,128)S(1)} %get-tuple-element.10.pv, f32[32,16,128]{2,1,0:T(8,128)S(1)} %get-tuple-element.11.g_row), custom_call_target="tpu_custom_call" | custom-call | tf_op jit(solution)/shard_map/finish/pallas_call | solution.py:429

commit v6 on v5

--- a/solution.py
+++ b/solution.py
@@ -327,6 +327,8 @@
     lanes = lax.broadcasted_iota(jnp.int32, (128, 128), 1)
     noise = jnp.where(rows == lanes, jnp.broadcast_to(vec[0], (128, 128)), 0.0)
     s_all = s_fin[...].reshape(128, 128) + noise
+    total(g_col, 7, gc_send, gc_recv).wait_recv()
+    g_c = jnp.transpose(g_col[...].reshape(128, 128))
     inverse = spd_inverse([s_all[i * PIVOTS : (i + 1) * PIVOTS] for i in range(M // PIVOTS)], PIVOTS)
 
     total(m_all, 3, ma_send, ma_recv).wait_recv()
@@ -334,8 +336,7 @@
     vectors_ref[0] = jnp.broadcast_to(vec[2] - mean, (8, 128))
     vectors_ref[1] = jnp.broadcast_to(vec[1], (8, 128))
 
-    total(g_col, 7, gc_send, gc_recv).wait_recv()
-    solved_ref[...] = mm(g_col[...].reshape(128, 128), inverse)
+    solved_ref[...] = mm(inverse, g_c)
 
     share.wait_recv()
 
@@ -366,14 +367,14 @@
 
 def finish(solved_ref, vectors_ref, pv, g_row, ana_hbm, post_hbm, ana, post, sem):
     solved = solved_ref[...]
-    ana[...] = (vectors_ref[1] + mm_nt(vectors_ref[0], solved))[0:1, :]
+    ana[...] = (vectors_ref[1] + mm(vectors_ref[0], solved))[0:1, :]
     copies = [pltpu.make_async_copy(ana, ana_hbm, sem.at[4])]
     copies[0].start()
     for j in range(4):
         first = (j % 2) * 16 + (j // 2) * 8
         g_j = g_row[first : first + 8].reshape(128, 128)
         here = slice(j * 128, (j + 1) * 128)
-        post[here, :] = pv[here, :] - mm_nt(g_j, solved)
+        post[here, :] = pv[here, :] - mm(g_j, solved)
         copies.append(pltpu.make_async_copy(post.at[here], post_hbm.at[here], sem.at[j]))
         copies[-1].start()
     for copy in copies:

time: 29.9 us -> 29.7 us (level)
    pallas_call x1, Pallas kernels: 1.44 us -> 1.12 us  [on_device(): pl.pallas_call(finish, name='finish', out_shape=(array(1, 128), array(512...]
where the time goes in v6:
time: 29.7 us; the launch traced here: 29.5 us
  Pallas kernels  28.9 us (97%)
  between operations  0.64 us (2%)
    pallas_call x1, Pallas kernels, on_device(): pl.pallas_call(kernel, name='analysis', out_shape=(array(128, 128), array...  27.8 us
    pallas_call x1, Pallas kernels, on_device(): pl.pallas_call(finish, name='finish', out_shape=(array(1, 128), array(512...  1.12 us

profile of v6, /device:TPU:1, one launch (start us, length us, event | category | flops | bytes accessed | tf_op | source)
XLA Modules:
  0.0 29.5 jit_solution(10519109286949363782)
XLA Ops:
  0.6 27.8 %analysis.1 = (f32[128,128]{1,0:T(8,128)S(1)}, f32[2,8,128]{2,1,0:T(8,128)S(1)}, f32[512,128]{1,0:T(8,128)S(1)}, f32[32,16,128]{2,1,0:T(8,128)S(1)}) custom-call(f32[512,128]{1,0:T(8,128)} %prior_hbm.1, f32[128,2048]{1,0:T(8,128)} %kernel_hbm.1, s32[128]{0:T(128)} %off_hbm.1, f32[1,128]{1,0:T(1,128)} %bitcast.4, f32[1,128]{1,0:T(1,128)} %bitcast.5, ...), custom_call_target="tpu_custom_call" | custom-call | tf_op jit(solution)/shard_map/analysis/pallas_call | solution.py:406
  28.4 1.1 %finish.1 = (f32[1,128]{1,0:T(1,128)}, f32[512,128]{1,0:T(8,128)}) custom-call(f32[128,128]{1,0:T(8,128)S(1)} %get-tuple-element.8.solved_ref, f32[2,8,128]{2,1,0:T(8,128)S(1)} %get-tuple-element.9.vectors_ref, f32[512,128]{1,0:T(8,128)S(1)} %get-tuple-element.10.pv, f32[32,16,128]{2,1,0:T(8,128)S(1)} %get-tuple-element.11.g_row), custom_call_target="tpu_custom_call" | custom-call | tf_op jit(solution)/shard_map/finish/pallas_call | solution.py:430

commit v7 on v6

--- a/solution.py
+++ b/solution.py
@@ -264,10 +264,10 @@
     g_col[r] = piece
     slot = core * 16 + y_hi * 8 + r
 
-    @pl.loop(1, 16)
-    def _(i):
-        to = (z * 2 + y_hi + i) % 16
-        send(g_sl.at[0], g_row.at[slot], gr_send, gr_recv, (z, (to // 2) * 4 + (to % 2) * 2 + core))
+    for dz in PLANES_STEPS + [0]:
+        for half in (0, 1) if dz else (1,):
+            col = (z + dz) % 8 * 4 + (y_hi + half) % 2 * 2 + core
+            send(g_sl.at[0], g_row.at[slot], gr_send, gr_recv, (z, col))
 
     @pl.when(z == r)
     def _():
@@ -367,14 +367,20 @@
 
 def finish(solved_ref, vectors_ref, pv, g_row, ana_hbm, post_hbm, ana, post, sem):
     solved = solved_ref[...]
-    ana[...] = (vectors_ref[1] + mm(vectors_ref[0], solved))[0:1, :]
-    copies = [pltpu.make_async_copy(ana, ana_hbm, sem.at[4])]
-    copies[0].start()
+    copies = []
     for j in range(4):
         first = (j % 2) * 16 + (j // 2) * 8
         g_j = g_row[first : first + 8].reshape(128, 128)
         here = slice(j * 128, (j + 1) * 128)
-        post[here, :] = pv[here, :] - mm(g_j, solved)
+        if j == 0:
+            both = mm(jnp.concatenate([vectors_ref[0], g_j], 0), solved)
+            change = both[8:, :]
+            ana[...] = (vectors_ref[1] + both[:8, :])[0:1, :]
+            copies.append(pltpu.make_async_copy(ana, ana_hbm, sem.at[4]))
+            copies[-1].start()
+        else:
+            change = mm(g_j, solved)
+        post[here, :] = pv[here, :] - change
         copies.append(pltpu.make_async_copy(post.at[here], post_hbm.at[here], sem.at[j]))
         copies[-1].start()
     for copy in copies:

time: 29.7 us -> 29.6 us (level)
  no operation moved by 1% of the time
where the time goes in v7:
time: 29.6 us; the launch traced here: 29.5 us
  Pallas kernels  28.8 us (97%)
  between operations  0.64 us (2%)
    pallas_call x1, Pallas kernels, on_device(): pl.pallas_call(kernel, name='analysis', out_shape=(array(128, 128), array...  27.7 us
    pallas_call x1, Pallas kernels, on_device(): pl.pallas_call(finish, name='finish', out_shape=(array(1, 128), array(512...  1.12 us

profile of v7, /device:TPU:1, one launch (start us, length us, event | category | flops | bytes accessed | tf_op | source)
XLA Modules:
  0.0 29.5 jit_solution(15360793269101760519)
XLA Ops:
  0.6 27.7 %analysis.1 = (f32[128,128]{1,0:T(8,128)S(1)}, f32[2,8,128]{2,1,0:T(8,128)S(1)}, f32[512,128]{1,0:T(8,128)S(1)}, f32[32,16,128]{2,1,0:T(8,128)S(1)}) custom-call(f32[512,128]{1,0:T(8,128)} %prior_hbm.1, f32[128,2048]{1,0:T(8,128)} %kernel_hbm.1, s32[128]{0:T(128)} %off_hbm.1, f32[1,128]{1,0:T(1,128)} %bitcast.4, f32[1,128]{1,0:T(1,128)} %bitcast.5, ...), custom_call_target="tpu_custom_call" | custom-call | tf_op jit(solution)/shard_map/analysis/pallas_call | solution.py:412
  28.3 1.1 %finish.1 = (f32[1,128]{1,0:T(1,128)}, f32[512,128]{1,0:T(8,128)}) custom-call(f32[128,128]{1,0:T(8,128)S(1)} %get-tuple-element.8.solved_ref, f32[2,8,128]{2,1,0:T(8,128)S(1)} %get-tuple-element.9.vectors_ref, f32[512,128]{1,0:T(8,128)S(1)} %get-tuple-element.10.pv, f32[32,16,128]{2,1,0:T(8,128)S(1)} %get-tuple-element.11.g_row), custom_call_target="tpu_custom_call" | custom-call | tf_op jit(solution)/shard_map/finish/pallas_call | solution.py:436

commit v8 on v7

--- a/solution.py
+++ b/solution.py
@@ -227,9 +227,8 @@
     g_src[...] = jnp.transpose(part).reshape(8, 16, 128)
     g_rs[r] = g_src[r]
 
-    @pl.loop(1, 8)
-    def _(i):
-        to = (r + i) % 8
+    for dx, flip in ((2, 1), (1, 1), (3, 1), (2, 0), (1, 0), (3, 0), (0, 1)):
+        to = (x + dx) % 4 * 2 + (r + flip) % 2
         send(g_src.at[to], g_rs.at[r], gs_send, gs_recv, (to, c))
 
     for copy in vec_copies:

time: 29.6 us -> 30 us (1.014)
  Pallas kernels: 28.8 us -> 29.2 us
    pallas_call x1, Pallas kernels: 27.7 us -> 28.1 us  [on_device(): pl.pallas_call(kernel, name='analysis', out_shape=(array(128, 128), array...]
where the time goes in v8:
time: 30 us; the launch traced here: 29.9 us
  Pallas kernels  29.2 us (97%)
  between operations  0.64 us (2%)
    pallas_call x1, Pallas kernels, on_device(): pl.pallas_call(kernel, name='analysis', out_shape=(array(128, 128), array...  28.1 us
    pallas_call x1, Pallas kernels, on_device(): pl.pallas_call(finish, name='finish', out_shape=(array(1, 128), array(512...  1.12 us

profile of v8, /device:TPU:1, one launch (start us, length us, event | category | flops | bytes accessed | tf_op | source)
XLA Modules:
  0.0 29.9 jit_solution(15471002766254840099)
XLA Ops:
  0.6 28.1 %analysis.1 = (f32[128,128]{1,0:T(8,128)S(1)}, f32[2,8,128]{2,1,0:T(8,128)S(1)}, f32[512,128]{1,0:T(8,128)S(1)}, f32[32,16,128]{2,1,0:T(8,128)S(1)}) custom-call(f32[512,128]{1,0:T(8,128)} %prior_hbm.1, f32[128,2048]{1,0:T(8,128)} %kernel_hbm.1, s32[128]{0:T(128)} %off_hbm.1, f32[1,128]{1,0:T(1,128)} %bitcast.4, f32[1,128]{1,0:T(1,128)} %bitcast.5, ...), custom_call_target="tpu_custom_call" | custom-call | tf_op jit(solution)/shard_map/analysis/pallas_call | solution.py:411
  28.8 1.1 %finish.1 = (f32[1,128]{1,0:T(1,128)}, f32[512,128]{1,0:T(8,128)}) custom-call(f32[128,128]{1,0:T(8,128)S(1)} %get-tuple-element.8.solved_ref, f32[2,8,128]{2,1,0:T(8,128)S(1)} %get-tuple-element.9.vectors_ref, f32[512,128]{1,0:T(8,128)S(1)} %get-tuple-element.10.pv, f32[32,16,128]{2,1,0:T(8,128)S(1)} %get-tuple-element.11.g_row), custom_call_target="tpu_custom_call" | custom-call | tf_op jit(solution)/shard_map/finish/pallas_call | solution.py:435
